TPU v7x, 512 devices: a whole 4x4x16 slice. The times are simulated.
512 devices in a mesh: grp: 16 (over y, z_hi, core), sub: 32 (over x, z_lo).
Axes of the slice: x: 4, y: 4, z: 16 (z_hi: 2, z_lo: 8; z = z_hi * 8 + z_lo), core: 2. Of those that a mesh axis runs over, the one named last changes fastest.
Arguments:
- activations: bfloat16 [262144, 2048], P(('grp', 'sub')), may hold values from -110 to 110
- norm_gain: float32 [2048], replicated, may hold values from 0.5 to 1.5
- key_weight: bfloat16 [2048, 768], P('sub'), may hold values from -0.125 to 0.125
- key_grads: bfloat16 [262144, 768], P(('grp', 'sub')), may hold values from -3 to 3
Outputs:
- input_grads: bfloat16 [262144, 2048], P(('grp', 'sub'))
- weight_grads: float32 [2048, 768], P('sub', 'grp')
- gain_grads: float32 [2048], P('sub')
All inputs are finite; a program needn't handle non-finite values.
Results may differ from a plain program's by a relative error of at most 0.0029.
Values may be sent and summed in bfloat16 or wider, within the bound.
A program may use at most 64 MiB of HBM per device.

v0:
```python
import jax
import jax.numpy as jnp
from jax import lax
from jax.sharding import PartitionSpec as P


def local(activations, norm_gain, key_weight, key_grads):
    inputs = activations.astype(jnp.float32)
    mean_square = jnp.mean(inputs * inputs, axis=1, keepdims=True)
    inverse_rms = lax.rsqrt(mean_square + 1e-05)
    normed = inputs * inverse_rms
    scaled = (normed * norm_gain).astype(jnp.bfloat16)
    grad_scaled = lax.dot_general(
        key_grads,
        lax.all_gather(key_weight, "sub", axis=0, tiled=True),
        (((1,), (1,)), ((), ())),
        preferred_element_type=jnp.float32,
    )
    gained = norm_gain * grad_scaled
    input_grads = (
        inverse_rms * (gained - normed * jnp.mean(gained * normed, axis=1, keepdims=True))
    ).astype(jnp.bfloat16)
    groups = lax.axis_size("grp")
    members = lax.axis_size("sub")
    feature_rows = key_weight.shape[0]
    key_width = key_grads.shape[1]
    term = lax.dot_general(
        scaled, key_grads, (((0,), (0,)), ((), ())), preferred_element_type=jnp.float32
    )
    received = lax.all_to_all(term, "sub", split_axis=0, concat_axis=1, tiled=True)
    shared = jnp.sum(received.reshape(feature_rows, members, key_width), axis=1)
    owned = lax.psum_scatter(shared, "grp", scatter_dimension=1, tiled=True)
    weight_grads = owned / groups
    local_gain = jnp.sum(grad_scaled * normed, axis=0)
    summed = lax.psum(local_gain, ("grp", "sub"))
    gain_sum = lax.dynamic_slice_in_dim(summed, lax.axis_index("sub") * feature_rows, feature_rows)
    gain_grads = gain_sum / groups
    return (input_grads, weight_grads, gain_grads)


def solution(mesh):
    return jax.shard_map(
        local,
        mesh=mesh,
        in_specs=(P(("grp", "sub"), None), P(), P("sub", None), P(("grp", "sub"), None)),
        out_specs=(P(("grp", "sub"), None), P("sub", "grp"), P("sub")),
        check_vma=False,
    )
```

profile of v0, /device:TPU:2, one launch (start us, length us, event | category | flops | bytes accessed | tf_op | source)
XLA Modules:
  0.0 569.9 jit_solution(18334966130599238533)
XLA Ops:
  8.0 0.0 copy-start
  8.0 2.1 fusion.10
  10.2 0.0 copy-done
  10.2 6.2 %fusion.11 = f32[2048,768]{1,0:T(8,128)} fusion(bf16[512,768]{1,0:T(8,128)(2,1)S(1)} %copy-done, bf16[512,2048]{1,0:T(8,128)(2,1)} %param.4, f32[2048]{0:T(1024)} %param.5, f32[512]{0:T(512)S(1)} %add_rsqrt_fusion), kind=kOutput, calls=%fused_computation.13 | convolution fusion | flops 1614807040 | bytes 9185280 | tf_op jit(solution)/shard_map/dot_general | solution.py:27
  16.4 0.0 copy-start.1
  16.4 0.0 copy-start.2
  16.4 15.9 %all-to-all-start = ((f32[32,64,768]{2,1,0:T(8,128)}), f32[32,64,768]{2,1,0:T(8,128)}, u32[]{:S(2)}, u32[]{:S(2)}) async-start(f32[32,64,768]{2,1,0:T(8,128)} %bitcast.6), calls=%async_computation | async-start | bytes 12582912 | tf_op jit(solution)/shard_map/all_to_all | solution.py:30
  32.2 0.0 all-gather.2.cloned.1.call-start
  32.3 0.7 all-gather.2.cloned.1.call-update
  33.0 0.0 reduce-scatter.4.cloned.1.call-start
  33.0 394.7 %all-gather.2.cloned.1.call-done = bf16[2048,768]{1,0:T(8,128)(2,1)} async-done(((bf16[64,768]{1,0:T(8,128)(2,1)}), bf16[2048,768]{1,0:T(8,128)(2,1)}) %all-gather.2.cloned.1.call-update) | async-done | bytes 3145744 | tf_op jit(solution)/shard_map/all_gather | solution.py:15
  427.7 0.0 copy-done.1
  427.7 0.0 copy-done.2
  427.7 6.0 %fusion.9 = (f32[2048]{0:T(1024)S(1)}, f32[512]{0:T(512)S(1)}, f32[512,2048]{1,0:T(8,128)}) fusion(bf16[512,2048]{1,0:T(8,128)(2,1)S(1)} %copy-done.1, f32[512]{0:T(512)S(1)} %add_rsqrt_fusion, f32[2048]{0:T(1024)S(1)} %copy-done.2, bf16[512,768]{1,0:T(8,128)(2,1)S(1)} %copy-done, bf16[2048,768]{1,0:T(8,128)(2,1)} %all-gather.2.cloned.1.call-done), kind=kOutput, calls=%fused_computation.11 | convolution fusion | flops 1617950208 | bytes 10244096 | tf_op jit(solution)/shard_map/dot_general | solution.py:13
  433.7 0.0 all-to-all-done
  433.7 3.1 reduce_sum.38
  436.8 0.9 copy.9
  437.7 0.0 reduce-scatter.4.cloned.1.call-update
  437.7 4.6 fusion.7
  442.3 118.0 %psum.7 = f32[2048]{0:T(1024)S(1)} all-reduce(f32[2048]{0:T(1024)S(1)} %get-tuple-element.9), channel_id=1, replica_groups=mesh['grp'=16,'sub'=32] {'grp','sub'}, use_global_device_ids=true, to_apply=%region_5.0 | all-reduce | flops 2048 | bytes 16384 | tf_op jit(solution)/shard_map/psum | solution.py:35
  560.3 0.6 dynamic-slice_multiply_fusion
  560.9 0.0 reduce-scatter.4.cloned.1.call-done
  560.9 0.8 copy.10
  561.7 0.7 copy.8
  (3 shorter events, 0.0 us)
Async XLA Ops:
  8.0 2.2 copy-start
  16.4 411.4 %copy-start.1 = (bf16[512,2048]{1,0:T(8,128)(2,1)S(1)}, bf16[512,2048]{1,0:T(8,128)(2,1)}, u32[]{:S(2)}) copy-start(bf16[512,2048]{1,0:T(8,128)(2,1)} %param.4) | copy-start | bytes 6291460
  16.4 411.4 %copy-start.2 = (f32[2048]{0:T(1024)S(1)}, f32[2048]{0:T(1024)}, u32[]{:S(2)}) copy-start(f32[2048]{0:T(1024)} %param.5) | copy-start | bytes 24580
  16.4 417.3 %all-to-all-start = ((f32[32,64,768]{2,1,0:T(8,128)}), f32[32,64,768]{2,1,0:T(8,128)}, u32[]{:S(2)}, u32[]{:S(2)}) async-start(f32[32,64,768]{2,1,0:T(8,128)} %bitcast.6), calls=%async_computation | async-start | bytes 12582912 | tf_op jit(solution)/shard_map/all_to_all | solution.py:30
  32.2 395.5 %all-gather.2.cloned.1.call-start = ((), (), s32[]{:S(2)}) async-start(), calls=%async_computation.2 | async-start | bytes 3244032 | tf_op jit(solution)/shard_map/all_gather | solution.py:15
  33.0 527.9 %reduce-scatter.4.cloned.1.call-start = ((), (), s32[]{:S(2)}) async-start(), calls=%async_computation.3 | async-start | bytes 417792
Sparse Core Ops, SparseCore 0:
  35.1 392.5 all-gather.1
Sparse Core Ops, SparseCore 1:
  437.8 106.9 reduce-scatter.3
where the time goes:
time: 570 us
  waiting for transfers between devices  395 us (69%)
  blocking collectives  118 us (21%)
  starting transfers between devices  15.9 us (3%)
  between operations  15.5 us (3%)
  matrix products  12.1 us (2%)
  other arithmetic  10.4 us (2%)
    all_gather x1, waiting for transfers between devices, local(): lax.all_gather(key_weight, 'sub', axis=0, tiled=True)  395 us
    psum x1, blocking collectives, local(): summed = lax.psum(local_gain, ('grp', 'sub'))  118 us
    all_to_all x1, starting transfers between devices, local(): lax.all_to_all(term, 'sub', split_axis=0, concat_axis=1, tiled=True)  15.9 us
  transfers between devices with their start and end apart: 3, of which 1 were waited for; matrix products, arithmetic and copies ran while one was open for 2% of the time, Pallas kernels for 0%

commit v1 on v0

--- a/solution.py
+++ b/solution.py
@@ -32,7 +32,7 @@
     owned = lax.psum_scatter(shared, "grp", scatter_dimension=1, tiled=True)
     weight_grads = owned / groups
     local_gain = jnp.sum(grad_scaled * normed, axis=0)
-    summed = lax.psum(local_gain, ("grp", "sub"))
+    summed = lax.psum(lax.psum(local_gain, "sub"), "grp")
     gain_sum = lax.dynamic_slice_in_dim(summed, lax.axis_index("sub") * feature_rows, feature_rows)
     gain_grads = gain_sum / groups
     return (input_grads, weight_grads, gain_grads)

time: 570 us -> 648 us (1.14)
  the two profiles are of different devices: /device:TPU:2 before, /device:TPU:1 now
where the time goes in v1:
time: 648 us; the launch traced here: 647 us
  waiting for transfers between devices  393 us (61%)
  blocking collectives  198 us (31%)
  starting transfers between devices  16.2 us (2%)
  between operations  15.5 us (2%)
  matrix products  12.1 us (2%)
  other arithmetic  10.5 us (2%)
    all_gather x1, waiting for transfers between devices, local(): lax.all_gather(key_weight, 'sub', axis=0, tiled=True)  392 us
    psum x2, blocking collectives, local(): summed = lax.psum(lax.psum(local_gain, 'sub'), 'grp')  198 us
    all_to_all x1, starting transfers between devices, local(): lax.all_to_all(term, 'sub', split_axis=0, concat_axis=1, tiled=True)  16.2 us
  transfers between devices with their start and end apart: 3, of which 1 were waited for; matrix products, arithmetic and copies ran while one was open for 2% of the time, Pallas kernels for 0%

profile of v1, /device:TPU:1, one launch (start us, length us, event | category | flops | bytes accessed | tf_op | source)
XLA Modules:
  0.0 647.4 jit_solution(6220572140583982227)
XLA Ops:
  8.0 0.0 copy-start
  8.0 2.1 fusion.10
  10.2 0.0 copy-done
  10.2 6.2 fusion.11
  16.4 0.0 copy-start.1
  16.4 0.0 copy-start.2
  16.4 16.2 %all-to-all-start = ((f32[32,64,768]{2,1,0:T(8,128)}), f32[32,64,768]{2,1,0:T(8,128)}, u32[]{:S(2)}, u32[]{:S(2)}) async-start(f32[32,64,768]{2,1,0:T(8,128)} %bitcast.6), calls=%async_computation | async-start | bytes 12582912 | tf_op jit(solution)/shard_map/all_to_all | solution.py:30
  32.5 0.0 all-gather.2.cloned.1.call-start
  32.6 0.7 all-gather.2.cloned.1.call-update
  33.3 0.0 reduce-scatter.4.cloned.1.call-start
  33.3 391.8 %all-gather.2.cloned.1.call-done = bf16[2048,768]{1,0:T(8,128)(2,1)} async-done(((bf16[64,768]{1,0:T(8,128)(2,1)}), bf16[2048,768]{1,0:T(8,128)(2,1)}) %all-gather.2.cloned.1.call-update) | async-done | bytes 3145744 | tf_op jit(solution)/shard_map/all_gather | solution.py:15
  425.2 0.0 copy-done.1
  425.2 0.0 copy-done.2
  425.2 6.0 fusion.9
  431.1 0.0 all-to-all-done
  431.1 3.1 reduce_sum.38
  434.2 0.9 copy.9
  435.1 0.0 reduce-scatter.4.cloned.1.call-update
  435.2 4.6 fusion.7
  439.7 106.7 %psum.14 = f32[2048]{0:T(1024)S(1)} all-reduce(f32[2048]{0:T(1024)S(1)} %get-tuple-element.9), channel_id=1, replica_groups=mesh['grp'=16,'sub'=32] {'sub'}, use_global_device_ids=true, to_apply=%region_5.0 | all-reduce | flops 2048 | bytes 16384 | tf_op jit(solution)/shard_map/psum | solution.py:35
  546.4 91.4 %psum.15 = f32[2048]{0:T(1024)S(1)} all-reduce(f32[2048]{0:T(1024)S(1)} %psum.14), channel_id=1, replica_groups=mesh['grp'=16,'sub'=32] {'grp'}, use_global_device_ids=true, to_apply=%region_6.0 | all-reduce | flops 2048 | bytes 16384 | tf_op jit(solution)/shard_map/psum | solution.py:35
  637.8 0.6 dynamic-slice_multiply_fusion
  638.4 0.0 reduce-scatter.4.cloned.1.call-done
  638.4 0.8 copy.10
  639.2 0.7 copy.8
  (3 shorter events, 0.0 us)
Async XLA Ops:
  8.0 2.2 copy-start
  16.4 408.8 %copy-start.1 = (bf16[512,2048]{1,0:T(8,128)(2,1)S(1)}, bf16[512,2048]{1,0:T(8,128)(2,1)}, u32[]{:S(2)}) copy-start(bf16[512,2048]{1,0:T(8,128)(2,1)} %param.4) | copy-start | bytes 6291460
  16.4 408.8 %copy-start.2 = (f32[2048]{0:T(1024)S(1)}, f32[2048]{0:T(1024)}, u32[]{:S(2)}) copy-start(f32[2048]{0:T(1024)} %param.5) | copy-start | bytes 24580
  16.4 414.7 %all-to-all-start = ((f32[32,64,768]{2,1,0:T(8,128)}), f32[32,64,768]{2,1,0:T(8,128)}, u32[]{:S(2)}, u32[]{:S(2)}) async-start(f32[32,64,768]{2,1,0:T(8,128)} %bitcast.6), calls=%async_computation | async-start | bytes 12582912 | tf_op jit(solution)/shard_map/all_to_all | solution.py:30
  32.5 392.6 %all-gather.2.cloned.1.call-start = ((), (), s32[]{:S(2)}) async-start(), calls=%async_computation.2 | async-start | bytes 3244032 | tf_op jit(solution)/shard_map/all_gather | solution.py:15
  33.3 605.1 %reduce-scatter.4.cloned.1.call-start = ((), (), s32[]{:S(2)}) async-start(), calls=%async_computation.3 | async-start | bytes 417792
Sparse Core Ops, SparseCore 0:
  35.4 389.6 all-gather.1
Sparse Core Ops, SparseCore 1:
  435.2 108.9 reduce-scatter.3
